TPU v7x, 32 devices: a whole 2x2x4 slice. The times are simulated.
32 devices in a mesh: ctx: 8 (over z, x), head: 4 (over y, core).
Axes of the slice: x: 2, y: 2, z: 4, core: 2. Of those that a mesh axis runs over, the one named last changes fastest.
Arguments:
- queries: bfloat16 [1024, 8192], P('ctx', 'head'), may hold values from -110 to 110
- key_heads: bfloat16 [1024, 1024], P('ctx'), may hold values from -4.61 to 4.61
- value_heads: bfloat16 [1024, 1024], P('ctx'), may hold values from -6 to 6
- span_order: int32 [16], replicated, may hold values from 0 to 15, each once
- block_mask: int32 [16, 16], replicated, may hold values 0 or 1
- mamba_in: bfloat16 [1024, 16384], P('ctx', 'head'), may hold values from -6 to 6
- gate_in: bfloat16 [1024, 16384], P('ctx', 'head'), may hold values from -6 to 6
- conv_weight: float32 [4, 16384], P(None, 'head'), may hold values from -3 to 3
- conv_bias: float32 [16384], P('head'), may hold values from -3 to 3
- low_weight: bfloat16 [16384, 512], P('head'), may hold values from -0.046875 to 0.046875
- bc_weight: bfloat16 [16384, 32], P('head'), may hold values from -0.046875 to 0.046875
- low_gain: float32 [512], replicated, may hold values from 0.1 to 1.9
- dt_weight: bfloat16 [512, 16384], P(None, 'head'), may hold values from -0.25 to 0.25
- dt_bias: float32 [16384], P('head'), may hold values from -7 to -2
- rate_log: float32 [16384, 16], P('head'), may hold values from -3 to 2.77
- skip_gain: float32 [16384], P('head'), may hold values from 0.5 to 1.5
Outputs:
- attn_out: bfloat16 [1024, 8192], P('ctx', 'head')
- mamba_out: bfloat16 [1024, 16384], P('ctx', 'head')
Inputs may be any that keep to these rules, and one draw needn't show every extreme that they name: `span_order`: each of the 16 span numbers stands in exactly one slot.
All inputs are finite; a program needn't handle non-finite values.
Results may differ from a plain program's by a relative error of at most 0.013.
Values may be sent and summed in bfloat16 or wider, within the bound.
No kernel may reach another device: no remote copies, remote signals or barrier semaphores. Data moves between devices by JAX's collectives and lax.ppermute only.
A program may use at most 192 MiB of HBM per device.

v0:
```python
import math
import jax
import jax.numpy as jnp
from jax import lax
from jax.sharding import PartitionSpec as P

HD = 128
STATE = 16
CONV = 4
NEG_FILL = -1e30


def prefix(shard, axis, join, neutral):
    place = lax.axis_index(axis)
    gathered = jax.tree.map(
        lambda a, kind: lax.all_gather(a.astype(kind), axis), shard, (jnp.bfloat16, jnp.bfloat16)
    )
    state = jax.tree.map(lambda a, e: jnp.zeros_like(a) + jnp.asarray(e, a.dtype), shard, neutral)

    def one(turn, state):
        return join(
            state,
            jax.tree.map(
                lambda a, own: lax.dynamic_index_in_dim(a, turn, 0, False).astype(own.dtype),
                gathered,
                shard,
            ),
        )

    return lax.fori_loop(0, place, one, state)


def passed_along(value, axis, steps):
    count = lax.axis_size(axis)
    first, last = (max(0, -steps), min(count, count - steps))
    return lax.ppermute(value, axis, [(source, source + steps) for source in range(first, last)])


def table_lookup(lookup_table, wanted):
    entries = lookup_table.shape[0]
    matches = wanted[:, None] == jnp.arange(entries, dtype=jnp.int32)[None, :]
    return jnp.sum(jnp.where(matches, lookup_table[None, :], 0), axis=1)


def attend(state, piece, context):
    queries4, query_pos, query_half, own_spans, mask_rows, span_order, half_rows = context
    key_piece, value_piece = piece
    piece_rows = key_piece.shape[0]
    row_ids = jnp.arange(piece_rows, dtype=jnp.int32)
    key_span = table_lookup(span_order, row_ids // half_rows)
    key_pos = key_span * half_rows + row_ids % half_rows
    entries = span_order.shape[0]
    picked = key_span[None, :, None] == jnp.arange(entries, dtype=jnp.int32)[None, None, :]
    granted = jnp.sum(jnp.where(picked, mask_rows[:, None, :], 0), axis=2)
    allowed = (granted == 1) | (key_span[None, :] == own_spans[:, None])
    allowed_rows = jnp.where(query_half[:, None] == 0, allowed[0][None, :], allowed[1][None, :])
    visible = allowed_rows & (key_pos[None, :] <= query_pos[:, None])
    local_kv = queries4.shape[1]
    key_split = key_piece.reshape(piece_rows, local_kv, HD)
    value_split = value_piece.reshape(piece_rows, local_kv, HD)
    scores = jnp.einsum(
        "rkgd,mkd->kgrm", queries4, key_split, preferred_element_type=jnp.float32
    ) * HD ** (-0.5)
    scores = jnp.where(visible[None, None], scores, NEG_FILL)
    running, totals, summed = state
    highest = jnp.maximum(running, jnp.max(scores, axis=3))
    weights = jnp.where(visible[None, None], jnp.exp(scores - highest[..., None]), 0.0)
    totals = jnp.sum(weights, axis=3)
    summed = jnp.einsum(
        "kgrm,mkd->kgrd",
        weights.astype(jnp.bfloat16),
        value_split,
        preferred_element_type=jnp.float32,
    )
    return (highest, totals, summed)


def attention(queries, key_heads, value_heads, span_order, block_mask):
    row_count = queries.shape[0]
    half_rows = row_count // 2
    head_devices = lax.axis_size("head")
    kv_count = key_heads.shape[1] // HD
    local_kv = max(1, kv_count // head_devices)
    query_local = queries.shape[1] // HD
    per_group = query_local // local_kv
    group_size = query_local * head_devices // kv_count
    kv_start = lax.axis_index("head") * query_local // group_size
    key_mine = lax.dynamic_slice_in_dim(key_heads, kv_start * HD, local_kv * HD, 1)
    value_mine = lax.dynamic_slice_in_dim(value_heads, kv_start * HD, local_kv * HD, 1)
    queries4 = queries.reshape(row_count, local_kv, per_group, HD)
    own_slot = lax.axis_index("ctx")
    own_spans = lax.dynamic_slice_in_dim(span_order, 2 * own_slot, 2)
    entries = span_order.shape[0]
    chosen = own_spans[:, None] == jnp.arange(entries, dtype=jnp.int32)[None, :]
    mask_rows = jnp.sum(jnp.where(chosen[:, :, None], block_mask[None], 0), axis=1)
    row_ids = jnp.arange(row_count, dtype=jnp.int32)
    query_half = row_ids // half_rows
    query_span = jnp.where(query_half == 0, own_spans[0], own_spans[1])
    query_pos = query_span * half_rows + row_ids % half_rows
    context = (queries4, query_pos, query_half, own_spans, mask_rows, span_order, half_rows)
    start_state = (
        jnp.full((local_kv, per_group, row_count), NEG_FILL, jnp.float32),
        jnp.zeros((local_kv, per_group, row_count), jnp.float32),
        jnp.zeros((local_kv, per_group, row_count, HD), jnp.float32),
    )
    highest, totals, summed = attend(
        start_state,
        (
            lax.all_gather(key_mine, "ctx", axis=0, tiled=True),
            lax.all_gather(value_mine, "ctx", axis=0, tiled=True),
        ),
        context,
    )
    result = summed / totals[..., None]
    return result.transpose(2, 0, 1, 3).reshape(row_count, -1).astype(jnp.bfloat16)


def link(earlier, later):
    return (earlier[0] * later[0], earlier[1] * later[0] + later[1])


def local_scan(step_dt, inputs_f, b_vals, c_vals, rate_table, carry_in, length):
    row_count, channels = step_dt.shape
    blocks = row_count // length
    decay_all = jnp.exp(step_dt[:, None, :] * rate_table[None])
    drive_all = (step_dt * inputs_f)[:, None, :] * b_vals[:, :, None]

    def one_block(state, packed):
        decay_block, drive_block, c_block = packed
        results = []
        for offset in range(length):
            state = decay_block[offset] * state + drive_block[offset]
            results.append(jnp.sum(state * c_block[offset][:, None], axis=0))
        return (state, jnp.stack(results, axis=0))

    packed = (
        decay_all.reshape(blocks, length, STATE, channels),
        drive_all.reshape(blocks, length, STATE, channels),
        c_vals.reshape(blocks, length, STATE),
    )
    last_state, outputs = lax.scan(one_block, carry_in, packed)
    return (last_state, outputs.reshape(row_count, channels))


def carry_across(through, own_end):
    return prefix(
        (through, own_end), "ctx", link, (jnp.ones_like(through), jnp.zeros_like(own_end))
    )[1]


def normalize(low_vals, low_gain):
    scale_inv = lax.rsqrt(jnp.mean(low_vals * low_vals, axis=1, keepdims=True) + 1e-06)
    return (low_vals * scale_inv * low_gain[None, :]).astype(jnp.bfloat16)


def mamba(
    mamba_in,
    gate_in,
    conv_weight,
    conv_bias,
    low_weight,
    bc_weight,
    low_gain,
    dt_weight,
    dt_bias,
    rate_log,
    skip_gain,
):
    row_count, channels = mamba_in.shape
    rim = passed_along(mamba_in[row_count - (CONV - 1) :], "ctx", 1)
    extended = jnp.concatenate([rim, mamba_in], axis=0)
    mixed = conv_bias[None, :] + sum(
        (
            conv_weight[offset][None, :] * extended[offset : offset + row_count].astype(jnp.float32)
            for offset in range(CONV)
        )
    )
    act_bf = jax.nn.silu(mixed).astype(jnp.bfloat16)
    low_part = jnp.dot(act_bf, low_weight, preferred_element_type=jnp.float32)
    bc_part = jnp.dot(act_bf, bc_weight, preferred_element_type=jnp.float32)
    low_sum, bc_sum = (
        lax.psum(low_part.astype(jnp.bfloat16), "head").astype(jnp.float32),
        lax.psum(bc_part.astype(jnp.bfloat16), "head").astype(jnp.float32),
    )
    normed = normalize(low_sum, low_gain)
    step_dt = jax.nn.softplus(
        jnp.dot(normed, dt_weight, preferred_element_type=jnp.float32) + dt_bias[None, :]
    )
    rate_table = -jnp.exp(rate_log).T
    inputs_f = act_bf.astype(jnp.float32)
    b_vals = bc_sum[:, :STATE]
    c_vals = bc_sum[:, STATE:]
    length = math.gcd(row_count, 32)
    empty = jnp.zeros((STATE, channels), jnp.float32)
    through = jnp.exp(rate_table * jnp.sum(step_dt, axis=0)[None, :])
    own_end = local_scan(step_dt, inputs_f, b_vals, c_vals, rate_table, empty, length)[0]
    entering = carry_across(through, own_end)
    outputs = local_scan(step_dt, inputs_f, b_vals, c_vals, rate_table, entering, length)[1]
    result = outputs + skip_gain[None, :] * inputs_f
    return (result * jax.nn.silu(gate_in.astype(jnp.float32))).astype(jnp.bfloat16)


def per_device(
    queries,
    key_heads,
    value_heads,
    span_order,
    block_mask,
    mamba_in,
    gate_in,
    conv_weight,
    conv_bias,
    low_weight,
    bc_weight,
    low_gain,
    dt_weight,
    dt_bias,
    rate_log,
    skip_gain,
):
    attn_out = attention(queries, key_heads, value_heads, span_order, block_mask)
    mamba_out = mamba(
        mamba_in,
        gate_in,
        conv_weight,
        conv_bias,
        low_weight,
        bc_weight,
        low_gain,
        dt_weight,
        dt_bias,
        rate_log,
        skip_gain,
    )
    return (attn_out, mamba_out)


def solution(mesh):
    in_specs = (
        P("ctx", "head"),
        P("ctx", None),
        P("ctx", None),
        P(),
        P(),
        P("ctx", "head"),
        P("ctx", "head"),
        P(None, "head"),
        P("head"),
        P("head", None),
        P("head", None),
        P(),
        P(None, "head"),
        P("head"),
        P("head", None),
        P("head"),
    )
    out_specs = (P("ctx", "head"), P("ctx", "head"))
    return jax.shard_map(
        per_device, mesh=mesh, in_specs=in_specs, out_specs=out_specs, check_vma=False
    )
```

profile of v0, /device:TPU:26, one launch (start us, length us, event | category | flops | bytes accessed | tf_op | source)
XLA Modules:
  0.0 294.0 jit_solution(15363560117941585995)
XLA Ops:
  8.1 1.3 collective-permute-start
  15.6 3.5 %multiply_convert_fusion = bf16[128,4096]{1,0:T(8,128)(2,1)S(1)} fusion(bf16[128,4096]{1,0:T(8,128)(2,1)} %param.27, bf16[3,4096]{1,0:T(4,128)(2,1)S(1)} %collective-permute-done, f32[4096]{0:T(1024)S(1)} %bitcast.1187, f32[4096]{0:T(1024)S(1)} %bitcast.1188, f32[4096]{0:T(1024)S(1)} %bitcast.1186, f32[4096]{0:T(1024)S(1)} %bitcast.1185, f32[4096]{0:T(1024)} %param.30), kind=kLoop, calls=%fused_computation.376 | loop fusion | flops 13631488 | bytes 2203648 | tf_op jit(solution)/shard_map/convert_element_type | solution.py:178
  19.2 4.0 %convolution_convert_fusion = bf16[128,512]{1,0:T(8,128)(2,1)} fusion(bf16[128,4096]{1,0:T(8,128)(2,1)S(1)} %multiply_convert_fusion, bf16[4096,512]{1,0:T(8,128)(2,1)} %param.31), kind=kOutput, calls=%fused_computation.380 | convolution fusion | flops 536936448 | bytes 5373952 | tf_op jit(solution)/shard_map/dot_general | solution.py:179
  23.6 7.1 %psum.15 = bf16[128,32]{0,1:T(8,128)(2,1)S(1)} all-reduce(bf16[128,32]{0,1:T(8,128)(2,1)S(1)} %convolution_convert_fusion.1), channel_id=1, replica_groups=mesh['ctx'=8,'head'=4] {'head'}, use_global_device_ids=true, to_apply=%region_8.9 | all-reduce | flops 4096 | bytes 16384 | tf_op jit(solution)/shard_map/psum | solution.py:183
  30.9 26.4 %all-reduce.2.cloned.1.call-done = bf16[128,512]{1,0:T(8,128)(2,1)} async-done(((bf16[128,512]{1,0:T(8,128)(2,1)}), bf16[128,512]{1,0:T(8,128)(2,1)}) %all-reduce.2.cloned.1.call-update) | async-done | bytes 131088 | tf_op jit(solution)/shard_map/psum | solution.py:182
  58.3 4.3 %convert_multiply_fusion.3 = (f32[128,4096]{1,0:T(8,128)S(1)}, f32[4096]{0:T(1024)S(1)}, f32[128,4096]{1,0:T(8,128)S(1)}) fusion(bf16[128,4096]{1,0:T(8,128)(2,1)S(1)} %multiply_convert_fusion, f32[4096]{0:T(1024)S(1)} %copy-done.27, bf16[512,4096]{1,0:T(8,128)(2,1)} %param.34, bf16[128,512]{1,0:T(8,128)(2,1)} %all-reduce.2.cloned.1.call-done, ...), kind=kOutput, calls=%fused_computation.369 | convolution fusion | flops 542371840 | bytes 9603584 | tf_op jit(solution)/shard_map/dot_general | solution.py:187
  62.5 11.3 %broadcast_multiply_fusion = f32[4,32,16,4096]{3,2,1,0:T(8,128)} fusion(f32[4,32,16]{2,1,0:T(8,128)S(1)} %bitcast.1184, f32[4,32,4096]{2,1,0:T(8,128)S(1)} %bitcast.1144), kind=kLoop, calls=%fused_computation.356 | loop fusion | flops 8388608 | bytes 35659776 | tf_op jit(solution)/shard_map/mul | solution.py:126
  73.8 11.3 %multiply_exponential_fusion = f32[4,32,16,4096]{3,2,1,0:T(8,128)} fusion(f32[16,4096]{1,0:T(8,128)S(1)} %negate_bitcast_fusion, f32[4,32,4096]{2,1,0:T(8,128)S(1)} %bitcast.1143), kind=kLoop, calls=%fused_computation.355 | loop fusion | flops 8388608 | bytes 35913728 | tf_op jit(solution)/shard_map/exp | solution.py:125
  85.1 26.6 %while.37 = (s32[]{:T(128)}, f32[16,4096]{1,0:T(8,128)S(1)}, f32[4,32,16,4096]{3,2,1,0:T(8,128)}, f32[4,32,16,4096]{3,2,1,0:T(8,128)}, s32[]{:T(128)}, /*index=5...) while((s32[]{:T(128)}, f32[16,4096]{1,0:T(8,128)S(1)}, ...), condition=%wide.region_10.11_spmd.clone, body=%wide.region_9.10_spmd.clone.sunk | while | flops 4259874 | bytes 17302328 | solution.py:141
  85.1 6.6 %fusion.246 = f32[16,4096]{1,0:T(8,128)S(1)} fusion(f32[4,32,16,4096]{3,2,1,0:T(8,128)} %get-tuple-element.640, s32[]{:T(128)} %get-tuple-element.600, s32[]{:T(128)S(6)} %add.959, s32[]{:T(128)S(6)} %add.960, s32[]{:T(128)S(6)} %add.961, s32[]{:T(128)S(6)} %add.962, s32[]{:T(128)S(6)} %add.963, s32[]{:T(128)S(6)} %add.964, s32[]{:T(128)S(6)} %add.965, ...), kind=kLoop, calls=%fused_computation.228.clone.1 | loop fusion | flops 4259840 | bytes 17301632 | tf_op jit(solution)/shard_map/while/body/eval_jaxpr/add | solution.py:132
  91.8 6.6 %fusion.246 = f32[16,4096]{1,0:T(8,128)S(1)} fusion(f32[4,32,16,4096]{3,2,1,0:T(8,128)} %get-tuple-element.640, s32[]{:T(128)} %get-tuple-element.600, s32[]{:T(128)S(6)} %add.959, s32[]{:T(128)S(6)} %add.960, s32[]{:T(128)S(6)} %add.961, s32[]{:T(128)S(6)} %add.962, s32[]{:T(128)S(6)} %add.963, s32[]{:T(128)S(6)} %add.964, s32[]{:T(128)S(6)} %add.965, ...), kind=kLoop, calls=%fused_computation.228.clone.1 | loop fusion | flops 4259840 | bytes 17301632 | tf_op jit(solution)/shard_map/while/body/eval_jaxpr/add | solution.py:132
  98.4 6.6 %fusion.246 = f32[16,4096]{1,0:T(8,128)S(1)} fusion(f32[4,32,16,4096]{3,2,1,0:T(8,128)} %get-tuple-element.640, s32[]{:T(128)} %get-tuple-element.600, s32[]{:T(128)S(6)} %add.959, s32[]{:T(128)S(6)} %add.960, s32[]{:T(128)S(6)} %add.961, s32[]{:T(128)S(6)} %add.962, s32[]{:T(128)S(6)} %add.963, s32[]{:T(128)S(6)} %add.964, s32[]{:T(128)S(6)} %add.965, ...), kind=kLoop, calls=%fused_computation.228.clone.1 | loop fusion | flops 4259840 | bytes 17301632 | tf_op jit(solution)/shard_map/while/body/eval_jaxpr/add | solution.py:132
  105.1 6.6 %fusion.246 = f32[16,4096]{1,0:T(8,128)S(1)} fusion(f32[4,32,16,4096]{3,2,1,0:T(8,128)} %get-tuple-element.640, s32[]{:T(128)} %get-tuple-element.600, s32[]{:T(128)S(6)} %add.959, s32[]{:T(128)S(6)} %add.960, s32[]{:T(128)S(6)} %add.961, s32[]{:T(128)S(6)} %add.962, s32[]{:T(128)S(6)} %add.963, s32[]{:T(128)S(6)} %add.964, s32[]{:T(128)S(6)} %add.965, ...), kind=kLoop, calls=%fused_computation.228.clone.1 | loop fusion | flops 4259840 | bytes 17301632 | tf_op jit(solution)/shard_map/while/body/eval_jaxpr/add | solution.py:132
  112.5 1.3 fusion.195
  114.9 26.7 %all_gather.18 = bf16[1024,256]{0,1:T(8,128)(2,1)S(1)} all-gather(bf16[128,256]{0,1:T(8,128)(2,1)S(1)} %copy.47), channel_id=1, replica_groups=mesh['ctx'=8,'head'=4] {'ctx'}, dimensions={0}, use_global_device_ids=true | all-gather | bytes 589824 | tf_op jit(solution)/shard_map/all_gather | solution.py:109
  141.6 4.7 %fusion.160 = (f32[2,8,128]{2,1,0:T(8,128)S(1)}, f32[2,1024,128,8]{2,1,3,0:T(8,128)}) fusion(pred[128,1024]{0,1:T(8,128)(4,1)S(1)} %compare_and_fusion, bf16[1024,2,128,1]{0,2,3,1:T(8,128)(2,1)S(1)} %bitcast.1146, bf16[128,2,8,128]{3,2,1,0:T(8,128)(2,1)S(1)} %bitcast.1145), kind=kOutput, calls=%fused_computation.359 | convolution fusion | flops 543160320 | bytes 9576448 | tf_op jit(solution)/shard_map/rkgd,mkd->kgrm/dot_general | solution.py:61
  147.0 31.7 %all_gather.19 = bf16[1024,256]{1,0:T(8,128)(2,1)S(1)} all-gather(bf16[128,256]{1,0:T(8,128)(2,1)S(1)} %constant_dynamic-slice_fusion.32), channel_id=1, replica_groups=mesh['ctx'=8,'head'=4] {'ctx'}, dimensions={0}, use_global_device_ids=true | all-gather | bytes 589824 | tf_op jit(solution)/shard_map/all_gather | solution.py:110
  178.9 4.7 %fusion.161 = f32[2,8,128]{2,1,0:T(8,128)S(1)} fusion(f32[2,1024,128,8]{2,1,3,0:T(8,128)} %get-tuple-element.279, f32[2,8,128]{2,1,0:T(8,128)S(1)} %broadcast_maximum_fusion, pred[128,1024]{0,1:T(8,128)(4,1)S(1)} %compare_and_fusion), kind=kLoop, calls=%fused_computation.361 | loop fusion | flops 10483712 | bytes 8536064 | tf_op jit(solution)/shard_map/reduce_sum | solution.py:68
  183.7 1.2 copy-done.2
  184.9 2.2 divide_convert_fusion
  188.8 5.2 %all-gather.5.cloned.1.call-done = bf16[128,4096]{1,0:T(8,128)(2,1)} async-done(((bf16[16,4096]{1,0:T(8,128)(2,1)}), bf16[128,4096]{1,0:T(8,128)(2,1)}) %all-gather.5.cloned.1.call-update) | async-done | bytes 1048592 | tf_op jit(solution)/shard_map/all_gather | solution.py:16
  194.0 7.6 %while.35 = (s32[]{:T(128)}, f32[16,4096]{1,0:T(8,128)S(1)}, s32[]{:T(128)}, bf16[8,16,4096]{2,1,0:T(8,128)(2,1)}, bf16[8,16,4096]{2,1,0:T(8,128)(2,1)}, /*index=5*/s32[]{:T(128)}, s32[]{:T(128)}, s32[]{:T(128)}) while((s32[]{:T(128)}, f32[16,4096]{1,0:T(8,128)S(1)}, s32[]{:T(128)}, bf16[8,16,4096]{2,1,0:T(8,128)(2,1)}, ...), condition=%wide.region_12.13_spmd, body=%wide.region_11.12_spmd.sunk | while | flops 262149 | bytes 786555 | solution.py:30
  201.6 81.9 %while.36 = (s32[]{:T(128)}, f32[16,4096]{1,0:T(8,128)S(1)}, f32[4,32,4096]{2,1,0:T(8,128)}, f32[4,32,16,4096]{3,2,1,0:T(8,128)}, f32[4,32,16,4096]{3,2,1,0:T(8,...) while((s32[]{:T(128)}, f32[16,4096]{1,0:T(8,128)S(1)}, ...), condition=%wide.region_46.47_spmd, body=%wide.region_13.46_spmd.sunk | while | flops 8388641 | bytes 36451320 | solution.py:141
  201.6 1.7 fusion.245
  204.5 1.6 fusion.244
  206.1 7.9 %multiply_reduce_fusion.49 = (f32[4096]{0:T(1024)S(1)}, f32[16,4096]{1,0:T(8,128)S(1)}, f32[16,4096]{1,0:T(8,128)}, f32[16,4096]{1,0:T(8,128)}, f32[16,4096]{1,0...) fusion(f32[16]{0:T(128)S(1)} %get-tuple-element.465, ...), kind=kLoop, calls=%fused_computation.131.clone.1 | loop fusion | flops 4321280 | bytes 25182400 | tf_op jit(solution)/shard_map/while/body/eval_jaxpr/reduce_sum | solution.py:133
  214.0 1.2 multiply_reduce_fusion.65
  215.3 1.2 multiply_reduce_fusion.64
  216.5 1.2 multiply_reduce_fusion.63
  222.1 1.6 fusion.245
  224.9 1.6 fusion.244
  226.5 7.9 %multiply_reduce_fusion.49 = (f32[4096]{0:T(1024)S(1)}, f32[16,4096]{1,0:T(8,128)S(1)}, f32[16,4096]{1,0:T(8,128)}, f32[16,4096]{1,0:T(8,128)}, f32[16,4096]{1,0...) fusion(f32[16]{0:T(128)S(1)} %get-tuple-element.465, ...), kind=kLoop, calls=%fused_computation.131.clone.1 | loop fusion | flops 4321280 | bytes 25182400 | tf_op jit(solution)/shard_map/while/body/eval_jaxpr/reduce_sum | solution.py:133
  234.5 1.2 multiply_reduce_fusion.65
  235.7 1.2 multiply_reduce_fusion.64
  236.9 1.2 multiply_reduce_fusion.63
  242.6 1.6 fusion.245
  245.4 1.6 fusion.244
  247.0 7.9 %multiply_reduce_fusion.49 = (f32[4096]{0:T(1024)S(1)}, f32[16,4096]{1,0:T(8,128)S(1)}, f32[16,4096]{1,0:T(8,128)}, f32[16,4096]{1,0:T(8,128)}, f32[16,4096]{1,0...) fusion(f32[16]{0:T(128)S(1)} %get-tuple-element.465, ...), kind=kLoop, calls=%fused_computation.131.clone.1 | loop fusion | flops 4321280 | bytes 25182400 | tf_op jit(solution)/shard_map/while/body/eval_jaxpr/reduce_sum | solution.py:133
  255.0 1.2 multiply_reduce_fusion.65
  256.2 1.2 multiply_reduce_fusion.64
  257.4 1.2 multiply_reduce_fusion.63
  263.0 1.6 fusion.245
  265.8 1.6 fusion.244
  267.4 7.9 %multiply_reduce_fusion.49 = (f32[4096]{0:T(1024)S(1)}, f32[16,4096]{1,0:T(8,128)S(1)}, f32[16,4096]{1,0:T(8,128)}, f32[16,4096]{1,0:T(8,128)}, f32[16,4096]{1,0...) fusion(f32[16]{0:T(128)S(1)} %get-tuple-element.465, ...), kind=kLoop, calls=%fused_computation.131.clone.1 | loop fusion | flops 4321280 | bytes 25182400 | tf_op jit(solution)/shard_map/while/body/eval_jaxpr/reduce_sum | solution.py:133
  275.4 1.2 multiply_reduce_fusion.65
  276.6 1.2 multiply_reduce_fusion.64
  277.8 1.2 multiply_reduce_fusion.63
  283.5 4.0 %fusion.168 = bf16[128,4096]{1,0:T(8,128)(2,1)} fusion(bf16[128,4096]{1,0:T(8,128)(2,1)} %copy-done.3, bf16[128,4096]{1,0:T(8,128)(2,1)} %param.28, f32[4,32,4096]{2,1,0:T(8,128)} %get-tuple-element.102, f32[4096]{0:T(1024)} %param.37), kind=kLoop, calls=%fused_computation.372 | loop fusion | flops 5242880 | bytes 5259264 | tf_op jit(solution)/shard_map/convert_element_type | solution.py:200
  (286 shorter events, 42.1 us)
Async XLA Ops:
  7.2 7.5 %copy-start = (bf16[128,1024]{1,0:T(8,128)(2,1)S(1)}, bf16[128,1024]{1,0:T(8,128)(2,1)}, u32[]{:S(2)}) copy-start(bf16[128,1024]{1,0:T(8,128)(2,1)} %param.23) | copy-start | bytes 786436
  7.2 50.0 %all-reduce.2.cloned.1.call-start = ((), (), s32[]{:S(2)}) async-start(), calls=%async_computation | async-start | bytes 262144 | tf_op jit(solution)/shard_map/psum | solution.py:182
  8.1 7.5 %collective-permute-start = (bf16[3,4096]{1,0:T(4,128)(2,1)S(1)}, bf16[3,4096]{1,0:T(4,128)(2,1)S(1)}, u32[]{:S(2)}, u32[]{:S(2)}) collective-permute-start(bf16[3,4096]{1,0:T(4,128)(2,1)S(1)} %slice.693), channel_id=1, source_target_pairs={{0,4},{4,8},{8,12},{12,16},{16,20},{20,24},{24,28},{1,5},{5,9},{9,... | collective-permute-start | bytes 73736 | tf_op jit(solution)/shard_map/ppermute | solution.py:36
  19.1 39.1 %copy-start.3 = (bf16[128,4096]{1,0:T(8,128)(2,1)}, bf16[128,4096]{1,0:T(8,128)(2,1)S(1)}, u32[]{:S(2)}) copy-start(bf16[128,4096]{1,0:T(8,128)(2,1)S(1)} %multiply_convert_fusion) | copy-start | bytes 3145732
  19.1 4.1 %copy-start.6 = (bf16[4096,32]{0,1:T(8,128)(2,1)S(1)}, bf16[4096,32]{0,1:T(8,128)(2,1)}, u32[]{:S(2)}) copy-start(bf16[4096,32]{0,1:T(8,128)(2,1)} %param.32) | copy-start | bytes 786436
  19.1 39.1 %copy-start.27 = (f32[4096]{0:T(1024)S(1)}, f32[4096]{0:T(1024)}, u32[]{:S(2)}) copy-start(f32[4096]{0:T(1024)} %param.35) | copy-start | bytes 49156
  19.1 39.1 %copy-start.28 = (f32[512]{0:T(512)S(1)}, f32[512]{0:T(512)}, u32[]{:S(2)}) copy-start(f32[512]{0:T(512)} %param.33) | copy-start | bytes 6148
  23.1 165.6 %all-gather.7.cloned.1.call-start = ((), (), s32[]{:S(2)}) async-start(), calls=%async_computation.2 | async-start | bytes 1179648 | tf_op jit(solution)/shard_map/all_gather | solution.py:16
  85.1 28.7 %copy-start.5 = (bf16[128,2048]{1,0:T(8,128)(2,1)S(1)}, bf16[128,2048]{1,0:T(8,128)(2,1)}, u32[]{:S(2)}) copy-start(bf16[128,2048]{1,0:T(8,128)(2,1)} %param.22) | copy-start | bytes 1572868
  112.4 81.5 %all-gather.5.cloned.1.call-start = ((), (), s32[]{:S(2)}) async-start(), calls=%async_computation.1 | async-start | bytes 1179648 | tf_op jit(solution)/shard_map/all_gather | solution.py:16
  141.6 4.7 %copy-start.4 = (f32[4096,16]{0,1:T(8,128)S(1)}, f32[4096,16]{0,1:T(8,128)}, u32[]{:S(2)}) copy-start(f32[4096,16]{0,1:T(8,128)} %param.36) | copy-start | bytes 786436
  178.9 6.0 %copy-start.2 = (f32[2,1024,128,8]{2,1,3,0:T(8,128)S(1)}, f32[2,1024,128,8]{2,1,3,0:T(8,128)}, u32[]{:S(2)}) copy-start(f32[2,1024,128,8]{2,1,3,0:T(8,128)} %get-tuple-element.279) | copy-start | bytes 25165828
  214.0 4.5 %copy-start.12 = (f32[16]{0:T(128)S(1)}, f32[16]{0:T(128)}, u32[]{:S(2)}) copy-start(f32[16]{0:T(128)} %get-tuple-element.529) | copy-start | bytes 196 | tf_op jit(solution)/shard_map/while
  214.0 4.5 %copy-start.13 = (f32[16]{0:T(128)S(1)}, f32[16]{0:T(128)}, u32[]{:S(2)}) copy-start(f32[16]{0:T(128)} %get-tuple-element.531) | copy-start | bytes 196 | tf_op jit(solution)/shard_map/while
  214.0 4.7 %copy-start.10 = (f32[16]{0:T(128)S(1)}, f32[16]{0:T(128)}, u32[]{:S(2)}) copy-start(f32[16]{0:T(128)} %get-tuple-element.523) | copy-start | bytes 196 | tf_op jit(solution)/shard_map/while
  214.0 4.7 %copy-start.11 = (f32[16]{0:T(128)S(1)}, f32[16]{0:T(128)}, u32[]{:S(2)}) copy-start(f32[16]{0:T(128)} %get-tuple-element.525) | copy-start | bytes 196 | tf_op jit(solution)/shard_map/while
  214.0 4.9 %copy-start.8 = (f32[16]{0:T(128)S(1)}, f32[16]{0:T(128)}, u32[]{:S(2)}) copy-start(f32[16]{0:T(128)} %get-tuple-element.517) | copy-start | bytes 196 | tf_op jit(solution)/shard_map/while
  214.0 4.9 %copy-start.9 = (f32[16]{0:T(128)S(1)}, f32[16]{0:T(128)}, u32[]{:S(2)}) copy-start(f32[16]{0:T(128)} %get-tuple-element.519) | copy-start | bytes 196 | tf_op jit(solution)/shard_map/while
  214.0 5.0 %copy-start.7 = (f32[16]{0:T(128)S(1)}, f32[16]{0:T(128)}, u32[]{:S(2)}) copy-start(f32[16]{0:T(128)} %get-tuple-element.513) | copy-start | bytes 196 | tf_op jit(solution)/shard_map/while
  215.2 4.0 %copy-start.25 = (f32[16]{0:T(128)S(1)}, f32[16]{0:T(128)}, u32[]{:S(2)}) copy-start(f32[16]{0:T(128)} %get-tuple-element.504) | copy-start | bytes 196 | tf_op jit(solution)/shard_map/while
  215.2 4.0 %copy-start.26 = (f32[16]{0:T(128)S(1)}, f32[16]{0:T(128)}, u32[]{:S(2)}) copy-start(f32[16]{0:T(128)} %get-tuple-element.506) | copy-start | bytes 196 | tf_op jit(solution)/shard_map/while
  234.4 4.5 %copy-start.12 = (f32[16]{0:T(128)S(1)}, f32[16]{0:T(128)}, u32[]{:S(2)}) copy-start(f32[16]{0:T(128)} %get-tuple-element.529) | copy-start | bytes 196 | tf_op jit(solution)/shard_map/while
  234.4 4.5 %copy-start.13 = (f32[16]{0:T(128)S(1)}, f32[16]{0:T(128)}, u32[]{:S(2)}) copy-start(f32[16]{0:T(128)} %get-tuple-element.531) | copy-start | bytes 196 | tf_op jit(solution)/shard_map/while
  234.4 4.7 %copy-start.10 = (f32[16]{0:T(128)S(1)}, f32[16]{0:T(128)}, u32[]{:S(2)}) copy-start(f32[16]{0:T(128)} %get-tuple-element.523) | copy-start | bytes 196 | tf_op jit(solution)/shard_map/while
  234.5 4.7 %copy-start.11 = (f32[16]{0:T(128)S(1)}, f32[16]{0:T(128)}, u32[]{:S(2)}) copy-start(f32[16]{0:T(128)} %get-tuple-element.525) | copy-start | bytes 196 | tf_op jit(solution)/shard_map/while
  234.5 4.9 %copy-start.8 = (f32[16]{0:T(128)S(1)}, f32[16]{0:T(128)}, u32[]{:S(2)}) copy-start(f32[16]{0:T(128)} %get-tuple-element.517) | copy-start | bytes 196 | tf_op jit(solution)/shard_map/while
  234.5 4.9 %copy-start.9 = (f32[16]{0:T(128)S(1)}, f32[16]{0:T(128)}, u32[]{:S(2)}) copy-start(f32[16]{0:T(128)} %get-tuple-element.519) | copy-start | bytes 196 | tf_op jit(solution)/shard_map/while
  234.5 5.0 %copy-start.7 = (f32[16]{0:T(128)S(1)}, f32[16]{0:T(128)}, u32[]{:S(2)}) copy-start(f32[16]{0:T(128)} %get-tuple-element.513) | copy-start | bytes 196 | tf_op jit(solution)/shard_map/while
  235.7 4.0 %copy-start.25 = (f32[16]{0:T(128)S(1)}, f32[16]{0:T(128)}, u32[]{:S(2)}) copy-start(f32[16]{0:T(128)} %get-tuple-element.504) | copy-start | bytes 196 | tf_op jit(solution)/shard_map/while
  235.7 4.0 %copy-start.26 = (f32[16]{0:T(128)S(1)}, f32[16]{0:T(128)}, u32[]{:S(2)}) copy-start(f32[16]{0:T(128)} %get-tuple-element.506) | copy-start | bytes 196 | tf_op jit(solution)/shard_map/while
  254.9 4.5 %copy-start.12 = (f32[16]{0:T(128)S(1)}, f32[16]{0:T(128)}, u32[]{:S(2)}) copy-start(f32[16]{0:T(128)} %get-tuple-element.529) | copy-start | bytes 196 | tf_op jit(solution)/shard_map/while
  254.9 4.5 %copy-start.13 = (f32[16]{0:T(128)S(1)}, f32[16]{0:T(128)}, u32[]{:S(2)}) copy-start(f32[16]{0:T(128)} %get-tuple-element.531) | copy-start | bytes 196 | tf_op jit(solution)/shard_map/while
  254.9 4.7 %copy-start.10 = (f32[16]{0:T(128)S(1)}, f32[16]{0:T(128)}, u32[]{:S(2)}) copy-start(f32[16]{0:T(128)} %get-tuple-element.523) | copy-start | bytes 196 | tf_op jit(solution)/shard_map/while
  254.9 4.7 %copy-start.11 = (f32[16]{0:T(128)S(1)}, f32[16]{0:T(128)}, u32[]{:S(2)}) copy-start(f32[16]{0:T(128)} %get-tuple-element.525) | copy-start | bytes 196 | tf_op jit(solution)/shard_map/while
  255.0 4.9 %copy-start.8 = (f32[16]{0:T(128)S(1)}, f32[16]{0:T(128)}, u32[]{:S(2)}) copy-start(f32[16]{0:T(128)} %get-tuple-element.517) | copy-start | bytes 196 | tf_op jit(solution)/shard_map/while
  255.0 4.9 %copy-start.9 = (f32[16]{0:T(128)S(1)}, f32[16]{0:T(128)}, u32[]{:S(2)}) copy-start(f32[16]{0:T(128)} %get-tuple-element.519) | copy-start | bytes 196 | tf_op jit(solution)/shard_map/while
  255.0 5.0 %copy-start.7 = (f32[16]{0:T(128)S(1)}, f32[16]{0:T(128)}, u32[]{:S(2)}) copy-start(f32[16]{0:T(128)} %get-tuple-element.513) | copy-start | bytes 196 | tf_op jit(solution)/shard_map/while
  256.2 4.0 %copy-start.25 = (f32[16]{0:T(128)S(1)}, f32[16]{0:T(128)}, u32[]{:S(2)}) copy-start(f32[16]{0:T(128)} %get-tuple-element.504) | copy-start | bytes 196 | tf_op jit(solution)/shard_map/while
  256.2 4.0 %copy-start.26 = (f32[16]{0:T(128)S(1)}, f32[16]{0:T(128)}, u32[]{:S(2)}) copy-start(f32[16]{0:T(128)} %get-tuple-element.506) | copy-start | bytes 196 | tf_op jit(solution)/shard_map/while
  275.3 4.5 %copy-start.12 = (f32[16]{0:T(128)S(1)}, f32[16]{0:T(128)}, u32[]{:S(2)}) copy-start(f32[16]{0:T(128)} %get-tuple-element.529) | copy-start | bytes 196 | tf_op jit(solution)/shard_map/while
  275.3 4.5 %copy-start.13 = (f32[16]{0:T(128)S(1)}, f32[16]{0:T(128)}, u32[]{:S(2)}) copy-start(f32[16]{0:T(128)} %get-tuple-element.531) | copy-start | bytes 196 | tf_op jit(solution)/shard_map/while
  275.4 4.7 %copy-start.10 = (f32[16]{0:T(128)S(1)}, f32[16]{0:T(128)}, u32[]{:S(2)}) copy-start(f32[16]{0:T(128)} %get-tuple-element.523) | copy-start | bytes 196 | tf_op jit(solution)/shard_map/while
  275.4 4.7 %copy-start.11 = (f32[16]{0:T(128)S(1)}, f32[16]{0:T(128)}, u32[]{:S(2)}) copy-start(f32[16]{0:T(128)} %get-tuple-element.525) | copy-start | bytes 196 | tf_op jit(solution)/shard_map/while
  275.4 4.9 %copy-start.8 = (f32[16]{0:T(128)S(1)}, f32[16]{0:T(128)}, u32[]{:S(2)}) copy-start(f32[16]{0:T(128)} %get-tuple-element.517) | copy-start | bytes 196 | tf_op jit(solution)/shard_map/while
  275.4 4.9 %copy-start.9 = (f32[16]{0:T(128)S(1)}, f32[16]{0:T(128)}, u32[]{:S(2)}) copy-start(f32[16]{0:T(128)} %get-tuple-element.519) | copy-start | bytes 196 | tf_op jit(solution)/shard_map/while
  275.4 5.0 %copy-start.7 = (f32[16]{0:T(128)S(1)}, f32[16]{0:T(128)}, u32[]{:S(2)}) copy-start(f32[16]{0:T(128)} %get-tuple-element.513) | copy-start | bytes 196 | tf_op jit(solution)/shard_map/while
  276.6 4.0 %copy-start.25 = (f32[16]{0:T(128)S(1)}, f32[16]{0:T(128)}, u32[]{:S(2)}) copy-start(f32[16]{0:T(128)} %get-tuple-element.504) | copy-start | bytes 196 | tf_op jit(solution)/shard_map/while
  276.6 4.0 %copy-start.26 = (f32[16]{0:T(128)S(1)}, f32[16]{0:T(128)}, u32[]{:S(2)}) copy-start(f32[16]{0:T(128)} %get-tuple-element.506) | copy-start | bytes 196 | tf_op jit(solution)/shard_map/while
  (45 other events, 79.7 us)
Sparse Core Ops, SparseCore 0:
  23.3 33.9 all-reduce.1
  112.6 39.1 all-gather.6
  153.9 39.9 all-gather.4
where the time goes:
time: 295 us; the launch traced here: 294 us
  other arithmetic  137 us (46%)
  blocking collectives  65.5 us (22%)
  waiting for transfers between devices  31.6 us (11%)
  local copies, waits for them, and re-layouts  27.7 us (9%)
  matrix products  15.5 us (5%)
  between operations  14.1 us (5%)
    reduce_sum x68, other arithmetic, one_block(): results.append(jnp.sum(state * c_block[offset][:, None], axis=0))  60.4 us
    all_gather x1, blocking collectives, attention(): lax.all_gather(value_mine, 'ctx', axis=0, tiled=True)  31.7 us
    all_gather x1, blocking collectives, attention(): lax.all_gather(key_mine, 'ctx', axis=0, tiled=True)  26.7 us
    add x4, other arithmetic, one_block(): state = decay_block[offset] * state + drive_block[offset]  26.5 us
    psum x1, waiting for transfers between devices, mamba(): lax.psum(low_part.astype(jnp.bfloat16), 'head').astype(jnp.float32)  26.4 us
    mul x8, local copies, waits for them, and re-layouts, one_block(): results.append(jnp.sum(state * c_block[offset][:, None], axis=0))  13.1 us
    exp x1, other arithmetic, local_scan(): decay_all = jnp.exp(step_dt[:, None, :] * rate_table[None])  11.3 us
    mul x1, other arithmetic, local_scan(): drive_all = (step_dt * inputs_f)[:, None, :] * b_vals[:, :, None]  11.3 us
  transfers between devices with their start and end apart: 4, of which 2 were waited for; matrix products, arithmetic and copies ran while one was open for 8% of the time, Pallas kernels for 0%

commit v1 on v0

--- a/solution.py
+++ b/solution.py
@@ -179,7 +179,7 @@
     low_part = jnp.dot(act_bf, low_weight, preferred_element_type=jnp.float32)
     bc_part = jnp.dot(act_bf, bc_weight, preferred_element_type=jnp.float32)
     low_sum, bc_sum = (
-        lax.psum(low_part.astype(jnp.bfloat16), "head").astype(jnp.float32),
+        jnp.sum(lax.all_gather(low_part.astype(jnp.bfloat16), "head"), axis=0).astype(jnp.float32),
         lax.psum(bc_part.astype(jnp.bfloat16), "head").astype(jnp.float32),
     )
     normed = normalize(low_sum, low_gain)

time: 295 us -> 277 us (0.939)
  waiting for transfers between devices: 31.6 us -> 6.76 us
  blocking collectives: 65.5 us -> 73.3 us
    psum x1 -> x0, waiting for transfers between devices: 26.4 us -> none  [mamba(): lax.psum(low_part.astype(jnp.bfloat16), 'head').astype(jnp.float32)]
    all_gather x0 -> x1, blocking collectives: none -> 7.2 us  [mamba(): lax.all_gather(low_part.astype(jnp.bfloat16), 'head')]
  transfers between devices with their start and end apart: 4 -> 3, of which waited for: 2 -> 1; matrix products, arithmetic and copies ran while one was open for 8% -> 8% of each run, Pallas kernels for 0% -> 0%
where the time goes in v1:
time: 277 us; the launch traced here: 276 us
  other arithmetic  136 us (49%)
  blocking collectives  73.3 us (26%)
  local copies, waits for them, and re-layouts  27.9 us (10%)
  matrix products  14.7 us (5%)
  between operations  14.4 us (5%)
  waiting for transfers between devices  6.76 us (2%)
    reduce_sum x68, other arithmetic, one_block(): results.append(jnp.sum(state * c_block[offset][:, None], axis=0))  60.4 us
    all_gather x1, blocking collectives, attention(): lax.all_gather(value_mine, 'ctx', axis=0, tiled=True)  31.7 us
    all_gather x1, blocking collectives, attention(): lax.all_gather(key_mine, 'ctx', axis=0, tiled=True)  27.6 us
    add x4, other arithmetic, one_block(): state = decay_block[offset] * state + drive_block[offset]  26.5 us
    mul x8, local copies, waits for them, and re-layouts, one_block(): results.append(jnp.sum(state * c_block[offset][:, None], axis=0))  13.1 us
    exp x1, other arithmetic, local_scan(): decay_all = jnp.exp(step_dt[:, None, :] * rate_table[None])  11.3 us
    mul x1, other arithmetic, local_scan(): drive_all = (step_dt * inputs_f)[:, None, :] * b_vals[:, :, None]  11.3 us
    add x7, other arithmetic, link(): return (earlier[0] * later[0], earlier[1] * later[0] + later[1])  7.45 us
  transfers between devices with their start and end apart: 3, of which 1 were waited for; matrix products, arithmetic and copies ran while one was open for 8% of the time, Pallas kernels for 0%

profile of v1, /device:TPU:26, one launch (start us, length us, event | category | flops | bytes accessed | tf_op | source)
XLA Modules:
  0.0 275.8 jit_solution(17478535288300803043)
XLA Ops:
  8.1 1.3 collective-permute-start
  15.7 3.5 %multiply_convert_fusion = bf16[128,4096]{1,0:T(8,128)(2,1)S(1)} fusion(bf16[128,4096]{1,0:T(8,128)(2,1)} %param.27, bf16[3,4096]{1,0:T(4,128)(2,1)S(1)} %collective-permute-done, f32[4096]{0:T(1024)S(1)} %bitcast.1189, f32[4096]{0:T(1024)S(1)} %bitcast.1190, f32[4096]{0:T(1024)S(1)} %bitcast.1188, f32[4096]{0:T(1024)S(1)} %bitcast.1187, f32[4096]{0:T(1024)} %param.30), kind=kLoop, calls=%fused_computation.376 | loop fusion | flops 13631488 | bytes 2203648 | tf_op jit(solution)/shard_map/convert_element_type | solution.py:178
  19.2 3.3 %convolution_convert_fusion = bf16[128,512]{1,0:T(8,128)(2,1)S(1)} fusion(bf16[128,4096]{1,0:T(8,128)(2,1)S(1)} %multiply_convert_fusion, bf16[4096,512]{1,0:T(8,128)(2,1)} %param.31), kind=kOutput, calls=%fused_computation.380 | convolution fusion | flops 536936448 | bytes 5373952 | tf_op jit(solution)/shard_map/dot_general | solution.py:179
  22.5 7.2 %all-gather = bf16[512,512]{1,0:T(8,128)(2,1)S(1)} all-gather(bf16[128,512]{1,0:T(8,128)(2,1)S(1)} %convolution_convert_fusion), channel_id=2, replica_groups=mesh['ctx'=8,'head'=4] {'head'}, dimensions={0}, use_global_device_ids=true | all-gather | bytes 655360 | tf_op jit(solution)/shard_map/all_gather | solution.py:182
  30.4 6.8 %psum.7 = bf16[128,32]{0,1:T(8,128)(2,1)S(1)} all-reduce(bf16[128,32]{0,1:T(8,128)(2,1)S(1)} %convolution_convert_fusion.1), channel_id=1, replica_groups=mesh['ctx'=8,'head'=4] {'head'}, use_global_device_ids=true, to_apply=%region_8.9 | all-reduce | flops 4096 | bytes 16384 | tf_op jit(solution)/shard_map/psum | solution.py:183
  37.3 4.2 %convert_multiply_fusion.3 = (f32[128,4096]{1,0:T(8,128)S(1)}, f32[4096]{0:T(1024)S(1)}, f32[128,4096]{1,0:T(8,128)S(1)}) fusion(bf16[128,4096]{1,0:T(8,128)(2,1)S(1)} %multiply_convert_fusion, f32[4096]{0:T(1024)S(1)} %copy-done.27, bf16[512,4096]{1,0:T(8,128)(2,1)} %param.34, bf16[128,512]{1,0:T(8,128)(2,1)S(1)} %reduce_sum.358, f32[512]{0:T(512)S(1)} %copy-done.28, ...), kind=kOutput, calls=%fused_computation.369 | convolution fusion | flops 542371840 | bytes 9603584 | tf_op jit(solution)/shard_map/dot_general | solution.py:187
  41.5 11.3 %broadcast_multiply_fusion = f32[4,32,16,4096]{3,2,1,0:T(8,128)} fusion(f32[4,32,16]{2,1,0:T(8,128)S(1)} %bitcast.1186, f32[4,32,4096]{2,1,0:T(8,128)S(1)} %bitcast.1145), kind=kLoop, calls=%fused_computation.356 | loop fusion | flops 8388608 | bytes 35659776 | tf_op jit(solution)/shard_map/mul | solution.py:126
  52.8 11.3 %multiply_exponential_fusion = f32[4,32,16,4096]{3,2,1,0:T(8,128)} fusion(f32[16,4096]{1,0:T(8,128)S(1)} %negate_bitcast_fusion, f32[4,32,4096]{2,1,0:T(8,128)S(1)} %bitcast.1144), kind=kLoop, calls=%fused_computation.355 | loop fusion | flops 8388608 | bytes 35913728 | tf_op jit(solution)/shard_map/exp | solution.py:125
  64.1 26.6 %while.37 = (s32[]{:T(128)}, f32[16,4096]{1,0:T(8,128)S(1)}, f32[4,32,16,4096]{3,2,1,0:T(8,128)}, f32[4,32,16,4096]{3,2,1,0:T(8,128)}, s32[]{:T(128)}, /*index=5...) while((s32[]{:T(128)}, f32[16,4096]{1,0:T(8,128)S(1)}, ...), condition=%wide.region_10.11_spmd.clone, body=%wide.region_9.10_spmd.clone.sunk | while | flops 4259874 | bytes 17302328 | solution.py:141
  64.1 6.6 %fusion.246 = f32[16,4096]{1,0:T(8,128)S(1)} fusion(f32[4,32,16,4096]{3,2,1,0:T(8,128)} %get-tuple-element.640, s32[]{:T(128)} %get-tuple-element.600, s32[]{:T(128)S(6)} %add.957, s32[]{:T(128)S(6)} %add.958, s32[]{:T(128)S(6)} %add.959, s32[]{:T(128)S(6)} %add.960, s32[]{:T(128)S(6)} %add.961, s32[]{:T(128)S(6)} %add.962, s32[]{:T(128)S(6)} %add.963, ...), kind=kLoop, calls=%fused_computation.228.clone.1 | loop fusion | flops 4259840 | bytes 17301632 | tf_op jit(solution)/shard_map/while/body/eval_jaxpr/add | solution.py:132
  70.7 6.6 %fusion.246 = f32[16,4096]{1,0:T(8,128)S(1)} fusion(f32[4,32,16,4096]{3,2,1,0:T(8,128)} %get-tuple-element.640, s32[]{:T(128)} %get-tuple-element.600, s32[]{:T(128)S(6)} %add.957, s32[]{:T(128)S(6)} %add.958, s32[]{:T(128)S(6)} %add.959, s32[]{:T(128)S(6)} %add.960, s32[]{:T(128)S(6)} %add.961, s32[]{:T(128)S(6)} %add.962, s32[]{:T(128)S(6)} %add.963, ...), kind=kLoop, calls=%fused_computation.228.clone.1 | loop fusion | flops 4259840 | bytes 17301632 | tf_op jit(solution)/shard_map/while/body/eval_jaxpr/add | solution.py:132
  77.4 6.6 %fusion.246 = f32[16,4096]{1,0:T(8,128)S(1)} fusion(f32[4,32,16,4096]{3,2,1,0:T(8,128)} %get-tuple-element.640, s32[]{:T(128)} %get-tuple-element.600, s32[]{:T(128)S(6)} %add.957, s32[]{:T(128)S(6)} %add.958, s32[]{:T(128)S(6)} %add.959, s32[]{:T(128)S(6)} %add.960, s32[]{:T(128)S(6)} %add.961, s32[]{:T(128)S(6)} %add.962, s32[]{:T(128)S(6)} %add.963, ...), kind=kLoop, calls=%fused_computation.228.clone.1 | loop fusion | flops 4259840 | bytes 17301632 | tf_op jit(solution)/shard_map/while/body/eval_jaxpr/add | solution.py:132
  84.1 6.6 %fusion.246 = f32[16,4096]{1,0:T(8,128)S(1)} fusion(f32[4,32,16,4096]{3,2,1,0:T(8,128)} %get-tuple-element.640, s32[]{:T(128)} %get-tuple-element.600, s32[]{:T(128)S(6)} %add.957, s32[]{:T(128)S(6)} %add.958, s32[]{:T(128)S(6)} %add.959, s32[]{:T(128)S(6)} %add.960, s32[]{:T(128)S(6)} %add.961, s32[]{:T(128)S(6)} %add.962, s32[]{:T(128)S(6)} %add.963, ...), kind=kLoop, calls=%fused_computation.228.clone.1 | loop fusion | flops 4259840 | bytes 17301632 | tf_op jit(solution)/shard_map/while/body/eval_jaxpr/add | solution.py:132
  91.5 1.3 fusion.195
  94.0 27.6 %all_gather.24 = bf16[1024,256]{0,1:T(8,128)(2,1)S(1)} all-gather(bf16[128,256]{0,1:T(8,128)(2,1)S(1)} %copy.47), channel_id=1, replica_groups=mesh['ctx'=8,'head'=4] {'ctx'}, dimensions={0}, use_global_device_ids=true | all-gather | bytes 589824 | tf_op jit(solution)/shard_map/all_gather | solution.py:109
  121.6 4.7 %fusion.160 = (f32[2,8,128]{2,1,0:T(8,128)S(1)}, f32[2,1024,128,8]{2,1,3,0:T(8,128)}) fusion(pred[128,1024]{0,1:T(8,128)(4,1)S(1)} %compare_and_fusion, bf16[1024,2,128,1]{0,2,3,1:T(8,128)(2,1)S(1)} %bitcast.1147, bf16[128,2,8,128]{3,2,1,0:T(8,128)(2,1)S(1)} %bitcast.1146), kind=kOutput, calls=%fused_computation.359 | convolution fusion | flops 543160320 | bytes 9576448 | tf_op jit(solution)/shard_map/rkgd,mkd->kgrm/dot_general | solution.py:61
  127.0 31.7 %all_gather.25 = bf16[1024,256]{1,0:T(8,128)(2,1)S(1)} all-gather(bf16[128,256]{1,0:T(8,128)(2,1)S(1)} %constant_dynamic-slice_fusion.32), channel_id=1, replica_groups=mesh['ctx'=8,'head'=4] {'ctx'}, dimensions={0}, use_global_device_ids=true | all-gather | bytes 589824 | tf_op jit(solution)/shard_map/all_gather | solution.py:110
  158.9 4.6 %fusion.161 = f32[2,8,128]{2,1,0:T(8,128)S(1)} fusion(f32[2,1024,128,8]{2,1,3,0:T(8,128)} %get-tuple-element.279, f32[2,8,128]{2,1,0:T(8,128)S(1)} %broadcast_maximum_fusion, pred[128,1024]{0,1:T(8,128)(4,1)S(1)} %compare_and_fusion), kind=kLoop, calls=%fused_computation.361 | loop fusion | flops 10483712 | bytes 8536064 | tf_op jit(solution)/shard_map/reduce_sum | solution.py:68
  163.5 1.4 copy-done.2
  164.8 2.2 divide_convert_fusion
  168.7 6.7 %all-gather.6.cloned.1.call-done = bf16[128,4096]{1,0:T(8,128)(2,1)} async-done(((bf16[16,4096]{1,0:T(8,128)(2,1)}), bf16[128,4096]{1,0:T(8,128)(2,1)}) %all-gather.6.cloned.1.call-update) | async-done | bytes 1048592 | tf_op jit(solution)/shard_map/all_gather | solution.py:16
  175.5 7.6 %while.35 = (s32[]{:T(128)}, f32[16,4096]{1,0:T(8,128)S(1)}, s32[]{:T(128)}, bf16[8,16,4096]{2,1,0:T(8,128)(2,1)}, bf16[8,16,4096]{2,1,0:T(8,128)(2,1)}, /*index=5*/s32[]{:T(128)}, s32[]{:T(128)}, s32[]{:T(128)}) while((s32[]{:T(128)}, f32[16,4096]{1,0:T(8,128)S(1)}, s32[]{:T(128)}, bf16[8,16,4096]{2,1,0:T(8,128)(2,1)}, ...), condition=%wide.region_12.13_spmd, body=%wide.region_11.12_spmd.sunk | while | flops 262149 | bytes 786555 | solution.py:30
  183.1 81.9 %while.36 = (s32[]{:T(128)}, f32[16,4096]{1,0:T(8,128)S(1)}, f32[4,32,4096]{2,1,0:T(8,128)}, f32[4,32,16,4096]{3,2,1,0:T(8,128)}, f32[4,32,16,4096]{3,2,1,0:T(8,...) while((s32[]{:T(128)}, f32[16,4096]{1,0:T(8,128)S(1)}, ...), condition=%wide.region_46.47_spmd, body=%wide.region_13.46_spmd.sunk | while | flops 8388641 | bytes 36451320 | solution.py:141
  183.1 1.7 fusion.245
  186.0 1.6 fusion.244
  187.6 7.9 %multiply_reduce_fusion.49 = (f32[4096]{0:T(1024)S(1)}, f32[16,4096]{1,0:T(8,128)S(1)}, f32[16,4096]{1,0:T(8,128)}, f32[16,4096]{1,0:T(8,128)}, f32[16,4096]{1,0...) fusion(f32[16]{0:T(128)S(1)} %get-tuple-element.465, ...), kind=kLoop, calls=%fused_computation.131.clone.1 | loop fusion | flops 4321280 | bytes 25182400 | tf_op jit(solution)/shard_map/while/body/eval_jaxpr/reduce_sum | solution.py:133
  195.6 1.2 multiply_reduce_fusion.65
  196.8 1.2 multiply_reduce_fusion.64
  198.0 1.2 multiply_reduce_fusion.63
  203.7 1.6 fusion.245
  206.4 1.6 fusion.244
  208.0 7.9 %multiply_reduce_fusion.49 = (f32[4096]{0:T(1024)S(1)}, f32[16,4096]{1,0:T(8,128)S(1)}, f32[16,4096]{1,0:T(8,128)}, f32[16,4096]{1,0:T(8,128)}, f32[16,4096]{1,0...) fusion(f32[16]{0:T(128)S(1)} %get-tuple-element.465, ...), kind=kLoop, calls=%fused_computation.131.clone.1 | loop fusion | flops 4321280 | bytes 25182400 | tf_op jit(solution)/shard_map/while/body/eval_jaxpr/reduce_sum | solution.py:133
  216.0 1.2 multiply_reduce_fusion.65
  217.2 1.2 multiply_reduce_fusion.64
  218.4 1.2 multiply_reduce_fusion.63
  224.1 1.6 fusion.245
  226.9 1.6 fusion.244
  228.5 7.9 %multiply_reduce_fusion.49 = (f32[4096]{0:T(1024)S(1)}, f32[16,4096]{1,0:T(8,128)S(1)}, f32[16,4096]{1,0:T(8,128)}, f32[16,4096]{1,0:T(8,128)}, f32[16,4096]{1,0...) fusion(f32[16]{0:T(128)S(1)} %get-tuple-element.465, ...), kind=kLoop, calls=%fused_computation.131.clone.1 | loop fusion | flops 4321280 | bytes 25182400 | tf_op jit(solution)/shard_map/while/body/eval_jaxpr/reduce_sum | solution.py:133
  236.5 1.2 multiply_reduce_fusion.65
  237.7 1.2 multiply_reduce_fusion.64
  238.9 1.2 multiply_reduce_fusion.63
  244.6 1.6 fusion.245
  247.3 1.6 fusion.244
  249.0 7.9 %multiply_reduce_fusion.49 = (f32[4096]{0:T(1024)S(1)}, f32[16,4096]{1,0:T(8,128)S(1)}, f32[16,4096]{1,0:T(8,128)}, f32[16,4096]{1,0:T(8,128)}, f32[16,4096]{1,0...) fusion(f32[16]{0:T(128)S(1)} %get-tuple-element.465, ...), kind=kLoop, calls=%fused_computation.131.clone.1 | loop fusion | flops 4321280 | bytes 25182400 | tf_op jit(solution)/shard_map/while/body/eval_jaxpr/reduce_sum | solution.py:133
  256.9 1.2 multiply_reduce_fusion.65
  258.1 1.2 multiply_reduce_fusion.64
  259.3 1.2 multiply_reduce_fusion.63
  265.0 4.0 %fusion.168 = bf16[128,4096]{1,0:T(8,128)(2,1)} fusion(bf16[128,4096]{1,0:T(8,128)(2,1)} %copy-done.3, bf16[128,4096]{1,0:T(8,128)(2,1)} %param.28, f32[4,32,4096]{2,1,0:T(8,128)} %get-tuple-element.102, f32[4096]{0:T(1024)} %param.37), kind=kLoop, calls=%fused_computation.372 | loop fusion | flops 5242880 | bytes 5259264 | tf_op jit(solution)/shard_map/convert_element_type | solution.py:200
  (285 shorter events, 41.3 us)
Async XLA Ops:
  7.2 7.6 %copy-start = (bf16[128,1024]{1,0:T(8,128)(2,1)S(1)}, bf16[128,1024]{1,0:T(8,128)(2,1)}, u32[]{:S(2)}) copy-start(bf16[128,1024]{1,0:T(8,128)(2,1)} %param.23) | copy-start | bytes 786436
  7.2 161.6 %all-gather.8.cloned.1.call-start = ((), (), s32[]{:S(2)}) async-start(), calls=%async_computation.1 | async-start | bytes 1179648 | tf_op jit(solution)/shard_map/all_gather | solution.py:16
  8.1 7.6 %collective-permute-start = (bf16[3,4096]{1,0:T(4,128)(2,1)S(1)}, bf16[3,4096]{1,0:T(4,128)(2,1)S(1)}, u32[]{:S(2)}, u32[]{:S(2)}) collective-permute-start(bf16[3,4096]{1,0:T(4,128)(2,1)S(1)} %slice.693), channel_id=1, source_target_pairs={{0,4},{4,8},{8,12},{12,16},{16,20},{20,24},{24,28},{1,5},{5,9},{9,... | collective-permute-start | bytes 73736 | tf_op jit(solution)/shard_map/ppermute | solution.py:36
  19.2 18.1 %copy-start.3 = (bf16[128,4096]{1,0:T(8,128)(2,1)}, bf16[128,4096]{1,0:T(8,128)(2,1)S(1)}, u32[]{:S(2)}) copy-start(bf16[128,4096]{1,0:T(8,128)(2,1)S(1)} %multiply_convert_fusion) | copy-start | bytes 3145732
  19.2 10.7 %copy-start.6 = (bf16[4096,32]{0,1:T(8,128)(2,1)S(1)}, bf16[4096,32]{0,1:T(8,128)(2,1)}, u32[]{:S(2)}) copy-start(bf16[4096,32]{0,1:T(8,128)(2,1)} %param.32) | copy-start | bytes 786436
  22.5 14.8 %copy-start.27 = (f32[4096]{0:T(1024)S(1)}, f32[4096]{0:T(1024)}, u32[]{:S(2)}) copy-start(f32[4096]{0:T(1024)} %param.35) | copy-start | bytes 49156
  22.5 14.8 %copy-start.28 = (f32[512]{0:T(512)S(1)}, f32[512]{0:T(512)}, u32[]{:S(2)}) copy-start(f32[512]{0:T(512)} %param.33) | copy-start | bytes 6148
  64.1 28.8 %copy-start.5 = (bf16[128,2048]{1,0:T(8,128)(2,1)S(1)}, bf16[128,2048]{1,0:T(8,128)(2,1)}, u32[]{:S(2)}) copy-start(bf16[128,2048]{1,0:T(8,128)(2,1)} %param.22) | copy-start | bytes 1572868
  91.4 84.0 %all-gather.6.cloned.1.call-start = ((), (), s32[]{:S(2)}) async-start(), calls=%async_computation | async-start | bytes 1179648 | tf_op jit(solution)/shard_map/all_gather | solution.py:16
  121.6 4.7 %copy-start.4 = (f32[4096,16]{0,1:T(8,128)S(1)}, f32[4096,16]{0,1:T(8,128)}, u32[]{:S(2)}) copy-start(f32[4096,16]{0,1:T(8,128)} %param.36) | copy-start | bytes 786436
  158.9 6.0 %copy-start.2 = (f32[2,1024,128,8]{2,1,3,0:T(8,128)S(1)}, f32[2,1024,128,8]{2,1,3,0:T(8,128)}, u32[]{:S(2)}) copy-start(f32[2,1024,128,8]{2,1,3,0:T(8,128)} %get-tuple-element.279) | copy-start | bytes 25165828
  195.5 4.5 %copy-start.12 = (f32[16]{0:T(128)S(1)}, f32[16]{0:T(128)}, u32[]{:S(2)}) copy-start(f32[16]{0:T(128)} %get-tuple-element.529) | copy-start | bytes 196 | tf_op jit(solution)/shard_map/while
  195.5 4.5 %copy-start.13 = (f32[16]{0:T(128)S(1)}, f32[16]{0:T(128)}, u32[]{:S(2)}) copy-start(f32[16]{0:T(128)} %get-tuple-element.531) | copy-start | bytes 196 | tf_op jit(solution)/shard_map/while
  195.5 4.7 %copy-start.10 = (f32[16]{0:T(128)S(1)}, f32[16]{0:T(128)}, u32[]{:S(2)}) copy-start(f32[16]{0:T(128)} %get-tuple-element.523) | copy-start | bytes 196 | tf_op jit(solution)/shard_map/while
  195.5 4.7 %copy-start.11 = (f32[16]{0:T(128)S(1)}, f32[16]{0:T(128)}, u32[]{:S(2)}) copy-start(f32[16]{0:T(128)} %get-tuple-element.525) | copy-start | bytes 196 | tf_op jit(solution)/shard_map/while
  195.5 4.9 %copy-start.8 = (f32[16]{0:T(128)S(1)}, f32[16]{0:T(128)}, u32[]{:S(2)}) copy-start(f32[16]{0:T(128)} %get-tuple-element.517) | copy-start | bytes 196 | tf_op jit(solution)/shard_map/while
  195.5 4.9 %copy-start.9 = (f32[16]{0:T(128)S(1)}, f32[16]{0:T(128)}, u32[]{:S(2)}) copy-start(f32[16]{0:T(128)} %get-tuple-element.519) | copy-start | bytes 196 | tf_op jit(solution)/shard_map/while
  195.5 5.0 %copy-start.7 = (f32[16]{0:T(128)S(1)}, f32[16]{0:T(128)}, u32[]{:S(2)}) copy-start(f32[16]{0:T(128)} %get-tuple-element.513) | copy-start | bytes 196 | tf_op jit(solution)/shard_map/while
  196.8 4.0 %copy-start.25 = (f32[16]{0:T(128)S(1)}, f32[16]{0:T(128)}, u32[]{:S(2)}) copy-start(f32[16]{0:T(128)} %get-tuple-element.504) | copy-start | bytes 196 | tf_op jit(solution)/shard_map/while
  196.8 4.0 %copy-start.26 = (f32[16]{0:T(128)S(1)}, f32[16]{0:T(128)}, u32[]{:S(2)}) copy-start(f32[16]{0:T(128)} %get-tuple-element.506) | copy-start | bytes 196 | tf_op jit(solution)/shard_map/while
  215.9 4.5 %copy-start.12 = (f32[16]{0:T(128)S(1)}, f32[16]{0:T(128)}, u32[]{:S(2)}) copy-start(f32[16]{0:T(128)} %get-tuple-element.529) | copy-start | bytes 196 | tf_op jit(solution)/shard_map/while
  215.9 4.5 %copy-start.13 = (f32[16]{0:T(128)S(1)}, f32[16]{0:T(128)}, u32[]{:S(2)}) copy-start(f32[16]{0:T(128)} %get-tuple-element.531) | copy-start | bytes 196 | tf_op jit(solution)/shard_map/while
  216.0 4.7 %copy-start.10 = (f32[16]{0:T(128)S(1)}, f32[16]{0:T(128)}, u32[]{:S(2)}) copy-start(f32[16]{0:T(128)} %get-tuple-element.523) | copy-start | bytes 196 | tf_op jit(solution)/shard_map/while
  216.0 4.7 %copy-start.11 = (f32[16]{0:T(128)S(1)}, f32[16]{0:T(128)}, u32[]{:S(2)}) copy-start(f32[16]{0:T(128)} %get-tuple-element.525) | copy-start | bytes 196 | tf_op jit(solution)/shard_map/while
  216.0 4.9 %copy-start.8 = (f32[16]{0:T(128)S(1)}, f32[16]{0:T(128)}, u32[]{:S(2)}) copy-start(f32[16]{0:T(128)} %get-tuple-element.517) | copy-start | bytes 196 | tf_op jit(solution)/shard_map/while
  216.0 4.9 %copy-start.9 = (f32[16]{0:T(128)S(1)}, f32[16]{0:T(128)}, u32[]{:S(2)}) copy-start(f32[16]{0:T(128)} %get-tuple-element.519) | copy-start | bytes 196 | tf_op jit(solution)/shard_map/while
  216.0 5.0 %copy-start.7 = (f32[16]{0:T(128)S(1)}, f32[16]{0:T(128)}, u32[]{:S(2)}) copy-start(f32[16]{0:T(128)} %get-tuple-element.513) | copy-start | bytes 196 | tf_op jit(solution)/shard_map/while
  217.2 4.0 %copy-start.25 = (f32[16]{0:T(128)S(1)}, f32[16]{0:T(128)}, u32[]{:S(2)}) copy-start(f32[16]{0:T(128)} %get-tuple-element.504) | copy-start | bytes 196 | tf_op jit(solution)/shard_map/while
  217.2 4.0 %copy-start.26 = (f32[16]{0:T(128)S(1)}, f32[16]{0:T(128)}, u32[]{:S(2)}) copy-start(f32[16]{0:T(128)} %get-tuple-element.506) | copy-start | bytes 196 | tf_op jit(solution)/shard_map/while
  236.4 4.5 %copy-start.12 = (f32[16]{0:T(128)S(1)}, f32[16]{0:T(128)}, u32[]{:S(2)}) copy-start(f32[16]{0:T(128)} %get-tuple-element.529) | copy-start | bytes 196 | tf_op jit(solution)/shard_map/while
  236.4 4.5 %copy-start.13 = (f32[16]{0:T(128)S(1)}, f32[16]{0:T(128)}, u32[]{:S(2)}) copy-start(f32[16]{0:T(128)} %get-tuple-element.531) | copy-start | bytes 196 | tf_op jit(solution)/shard_map/while
  236.4 4.7 %copy-start.10 = (f32[16]{0:T(128)S(1)}, f32[16]{0:T(128)}, u32[]{:S(2)}) copy-start(f32[16]{0:T(128)} %get-tuple-element.523) | copy-start | bytes 196 | tf_op jit(solution)/shard_map/while
  236.5 4.7 %copy-start.11 = (f32[16]{0:T(128)S(1)}, f32[16]{0:T(128)}, u32[]{:S(2)}) copy-start(f32[16]{0:T(128)} %get-tuple-element.525) | copy-start | bytes 196 | tf_op jit(solution)/shard_map/while
  236.5 4.9 %copy-start.8 = (f32[16]{0:T(128)S(1)}, f32[16]{0:T(128)}, u32[]{:S(2)}) copy-start(f32[16]{0:T(128)} %get-tuple-element.517) | copy-start | bytes 196 | tf_op jit(solution)/shard_map/while
  236.5 4.9 %copy-start.9 = (f32[16]{0:T(128)S(1)}, f32[16]{0:T(128)}, u32[]{:S(2)}) copy-start(f32[16]{0:T(128)} %get-tuple-element.519) | copy-start | bytes 196 | tf_op jit(solution)/shard_map/while
  236.5 5.0 %copy-start.7 = (f32[16]{0:T(128)S(1)}, f32[16]{0:T(128)}, u32[]{:S(2)}) copy-start(f32[16]{0:T(128)} %get-tuple-element.513) | copy-start | bytes 196 | tf_op jit(solution)/shard_map/while
  237.7 4.0 %copy-start.25 = (f32[16]{0:T(128)S(1)}, f32[16]{0:T(128)}, u32[]{:S(2)}) copy-start(f32[16]{0:T(128)} %get-tuple-element.504) | copy-start | bytes 196 | tf_op jit(solution)/shard_map/while
  237.7 4.0 %copy-start.26 = (f32[16]{0:T(128)S(1)}, f32[16]{0:T(128)}, u32[]{:S(2)}) copy-start(f32[16]{0:T(128)} %get-tuple-element.506) | copy-start | bytes 196 | tf_op jit(solution)/shard_map/while
  256.8 4.5 %copy-start.12 = (f32[16]{0:T(128)S(1)}, f32[16]{0:T(128)}, u32[]{:S(2)}) copy-start(f32[16]{0:T(128)} %get-tuple-element.529) | copy-start | bytes 196 | tf_op jit(solution)/shard_map/while
  256.9 4.5 %copy-start.13 = (f32[16]{0:T(128)S(1)}, f32[16]{0:T(128)}, u32[]{:S(2)}) copy-start(f32[16]{0:T(128)} %get-tuple-element.531) | copy-start | bytes 196 | tf_op jit(solution)/shard_map/while
  256.9 4.7 %copy-start.10 = (f32[16]{0:T(128)S(1)}, f32[16]{0:T(128)}, u32[]{:S(2)}) copy-start(f32[16]{0:T(128)} %get-tuple-element.523) | copy-start | bytes 196 | tf_op jit(solution)/shard_map/while
  256.9 4.7 %copy-start.11 = (f32[16]{0:T(128)S(1)}, f32[16]{0:T(128)}, u32[]{:S(2)}) copy-start(f32[16]{0:T(128)} %get-tuple-element.525) | copy-start | bytes 196 | tf_op jit(solution)/shard_map/while
  256.9 4.9 %copy-start.8 = (f32[16]{0:T(128)S(1)}, f32[16]{0:T(128)}, u32[]{:S(2)}) copy-start(f32[16]{0:T(128)} %get-tuple-element.517) | copy-start | bytes 196 | tf_op jit(solution)/shard_map/while
  256.9 4.9 %copy-start.9 = (f32[16]{0:T(128)S(1)}, f32[16]{0:T(128)}, u32[]{:S(2)}) copy-start(f32[16]{0:T(128)} %get-tuple-element.519) | copy-start | bytes 196 | tf_op jit(solution)/shard_map/while
  256.9 5.0 %copy-start.7 = (f32[16]{0:T(128)S(1)}, f32[16]{0:T(128)}, u32[]{:S(2)}) copy-start(f32[16]{0:T(128)} %get-tuple-element.513) | copy-start | bytes 196 | tf_op jit(solution)/shard_map/while
  258.1 4.0 %copy-start.25 = (f32[16]{0:T(128)S(1)}, f32[16]{0:T(128)}, u32[]{:S(2)}) copy-start(f32[16]{0:T(128)} %get-tuple-element.504) | copy-start | bytes 196 | tf_op jit(solution)/shard_map/while
  258.1 4.0 %copy-start.26 = (f32[16]{0:T(128)S(1)}, f32[16]{0:T(128)}, u32[]{:S(2)}) copy-start(f32[16]{0:T(128)} %get-tuple-element.506) | copy-start | bytes 196 | tf_op jit(solution)/shard_map/while
  265.0 4.0 %copy-start.1 = (bf16[128,1024]{1,0:T(8,128)(2,1)S(1)}, bf16[128,1024]{1,0:T(8,128)(2,1)}, u32[]{:S(2)}) copy-start(bf16[128,1024]{1,0:T(8,128)(2,1)} %param.23) | copy-start | bytes 786436
  (44 other events, 75.7 us)
Sparse Core Ops, SparseCore 0:
  91.5 41.4 all-gather.7
  135.2 40.2 all-gather.5
